TPU v7x, 32 devices: a whole 2x2x4 slice. The times are simulated.
32 devices in a mesh: groups: 2 (over y), node: 4 (over z), rep: 4 (over x, core).
Axes of the slice: x: 2, y: 2, z: 4, core: 2. Of those that a mesh axis runs over, the one named last changes fastest.
Arguments:
- node_states: bfloat16 [8, 512, 512], P(('groups', 'rep'), 'node'), parts along dimension 0, may hold values from -6 to 6
- cotangent: bfloat16 [8, 512, 512], P(('groups', 'rep'), 'node'), parts along dimension 0, may hold values from -1.1953125 to 1.1953125
- reach_blocks: int32 [8, 8, 8], P(('groups', 'rep'), 'node'), parts along dimension 0, may hold values from 0 to 7, as said below
- reach_count: int32 [8, 8], P(('groups', 'rep'), 'node'), parts along dimension 0, may hold values from 1 to 8, as said below
- level_start: int32 [8, 17], P(('groups', 'rep')), parts along dimension 0, may hold values from 0 to 512, as said below
- query_weight: bfloat16 [512, 256], replicated, may hold values from -0.25 to 0.25
- key_weight: bfloat16 [512, 256], replicated, may hold values from -0.25 to 0.25
- value_weight: bfloat16 [512, 256], replicated, may hold values from -0.25 to 0.25
- out_weight: bfloat16 [256, 512], replicated, may hold values from -0.375 to 0.375
- bias_table: float32 [4, 32], replicated, may hold values from -4 to 412
Outputs:
- updated: bfloat16 [8, 512, 512], P(('groups', 'rep'), 'node'), parts along dimension 0
- node_state_gradient: bfloat16 [8, 512, 512], P(('groups', 'rep'), 'node'), parts along dimension 0
- grad_query: float32 [1024, 256], P('groups'), parts along dimension 0
- grad_key: float32 [1024, 256], P('groups'), parts along dimension 0
- grad_value: float32 [1024, 256], P('groups'), parts along dimension 0
- grad_out: float32 [512, 512], P('groups'), parts along dimension 0
There are 2 independent parts, one for each index of `groups`. A program takes and returns all parts, laid end to end along the dimension named above; an argument that names none is the same for every part. Nothing has to cross between parts.
Inputs may be any that keep to these rules, and one draw needn't show every extreme that they name: `reach_blocks`: in row b of a graph, entry 0 is b, entries 1 to min(b, 7) are distinct blocks below b, and any later entries are b. `reach_count`: row b holds at most b + 1; row 7 of every graph holds 8. `level_start`: strictly increasing; entry 0 is 0 and entry 16 is 512.
All inputs are finite; a program needn't handle non-finite values.
Results may differ from a plain program's by a relative error of at most 0.011.
Values may be sent and summed in bfloat16 or wider, within the bound.
No kernel may reach another device: no remote copies, remote signals or barrier semaphores. Data moves between devices by JAX's collectives and lax.ppermute only.
A program may use at most 64 MiB of HBM per device.

v0:
```python
import jax
import jax.numpy as jnp
from jax import lax
from jax.sharding import PartitionSpec as P

HEADS = 4
HEAD = 64
BLOCK = 64
DIST = 32
EPS = 1e-05
NEG = -1e30
HIGH = lax.Precision.HIGHEST
CONTRACT_ROWS = (((0,), (0,)), ((), ()))
CONTRACT_COLS = (((1,), (1,)), ((), ()))


def rows_product(left, right):
    return lax.dot_general(left, right, CONTRACT_ROWS, preferred_element_type=jnp.float32)


def cols_product(left, right):
    return lax.dot_general(left, right, CONTRACT_COLS, preferred_element_type=jnp.float32)


def expand(listed):
    return jnp.repeat(jnp.repeat(listed, BLOCK, axis=0), BLOCK, axis=1)


def level_tables(starts, total, bias_table):
    level_count = starts.shape[0] - 1
    places = jnp.arange(total, dtype=jnp.int32)
    inner = starts[1:level_count]
    levels = jnp.sum((places[:, None] >= inner[None, :]).astype(jnp.int32), axis=1)
    marks = jnp.arange(level_count, dtype=jnp.int32)
    onehot = (levels[:, None] == marks[None, :]).astype(jnp.float32)
    spread = jnp.clip(marks[:, None] - marks[None, :], 0, DIST - 1)
    picks = (spread[:, :, None] == jnp.arange(DIST, dtype=jnp.int32)[None, None, :]).astype(
        jnp.float32
    )
    level_bias = jnp.einsum("hd,abd->hab", bias_table, picks, precision=HIGH)
    return (levels, onehot, level_bias)


def bias_block(row_onehot, head_bias, col_onehot):
    row_part = jnp.dot(row_onehot, head_bias, precision=HIGH)
    return lax.dot_general(row_part, col_onehot, CONTRACT_COLS, precision=HIGH)


def on_device(
    node_states,
    cotangent,
    reach_blocks,
    reach_count,
    level_start,
    query_weight,
    key_weight,
    value_weight,
    out_weight,
    bias_table,
):
    states = node_states[0]
    grads_in = cotangent[0]
    blocks = reach_blocks[0]
    counts = reach_count[0]
    starts = level_start[0]
    rows_dev = states.shape[0]
    width = query_weight.shape[1]
    total = rows_dev * lax.axis_size("node")
    offset = lax.axis_index("node") * rows_dev
    scale = HEAD ** (-0.5)
    key_blocks = total // BLOCK
    states_single_float = states.astype(jnp.float32)
    inverse_norm_scale = lax.rsqrt(
        jnp.mean(states_single_float * states_single_float, axis=1, keepdims=True) + EPS
    )
    centered_states = states_single_float * inverse_norm_scale
    normalized_states = centered_states.astype(jnp.bfloat16)
    queries = jnp.dot(normalized_states, query_weight, preferred_element_type=jnp.float32).astype(
        jnp.bfloat16
    )
    keys = jnp.dot(normalized_states, key_weight, preferred_element_type=jnp.float32).astype(
        jnp.bfloat16
    )
    values = jnp.dot(normalized_states, value_weight, preferred_element_type=jnp.float32).astype(
        jnp.bfloat16
    )
    keys_all, values_all = (
        lax.all_gather(keys, "node", axis=0, tiled=True),
        lax.all_gather(values, "node", axis=0, tiled=True),
    )
    levels, onehot, level_bias = level_tables(starts, total, bias_table)
    positions = jnp.arange(total, dtype=jnp.int32)
    local = jnp.arange(rows_dev, dtype=jnp.int32)
    row_ids = offset + local
    row_levels = lax.dynamic_slice_in_dim(levels, offset, rows_dev, 0)
    row_onehot = lax.dynamic_slice_in_dim(onehot, offset, rows_dev, 0)
    slots = jnp.arange(blocks.shape[1], dtype=jnp.int32)
    live = slots[None, :] < counts[:, None]
    kinds = jnp.arange(key_blocks, dtype=jnp.int32)
    listed = jnp.any((blocks[:, :, None] == kinds[None, None, :]) & live[:, :, None], axis=1)
    visible = expand(listed) & (
        (levels[None, :] < row_levels[:, None]) | (positions[None, :] == row_ids[:, None])
    )
    prob_list = []
    lse_list = []
    mixed_list = []
    for head in range(HEADS):
        lower = head * HEAD
        scores = (
            cols_product(queries[:, lower : lower + HEAD], keys_all[:, lower : lower + HEAD])
            * scale
        )
        scores = scores + bias_block(row_onehot, level_bias[head], onehot)
        scores = jnp.where(visible, scores, NEG)
        peak = jnp.max(scores, axis=1, keepdims=True)
        mass = jnp.sum(jnp.where(visible, jnp.exp(scores - peak), 0.0), axis=1, keepdims=True)
        lse = peak + jnp.log(mass)
        probs = jnp.where(visible, jnp.exp(scores - lse), 0.0).astype(jnp.bfloat16)
        prob_list.append(probs)
        lse_list.append(lse)
        mixed_list.append(
            jnp.dot(probs, values_all[:, lower : lower + HEAD], preferred_element_type=jnp.float32)
        )
    mixed = jnp.concatenate(mixed_list, axis=1).astype(jnp.bfloat16)
    updated = (
        states_single_float + jnp.dot(mixed, out_weight, preferred_element_type=jnp.float32)
    ).astype(jnp.bfloat16)
    partial_out = rows_product(mixed, grads_in)
    d_mixed = cols_product(grads_in, out_weight).astype(jnp.bfloat16)
    score_grads = []
    delta_list = []
    query_grads = []
    for head in range(HEADS):
        lower = head * HEAD
        mixed_head = d_mixed[:, lower : lower + HEAD]
        delta = jnp.sum(
            mixed_head.astype(jnp.float32) * mixed[:, lower : lower + HEAD].astype(jnp.float32),
            axis=1,
            keepdims=True,
        )
        d_probs = cols_product(mixed_head, values_all[:, lower : lower + HEAD])
        d_scores = (prob_list[head].astype(jnp.float32) * (d_probs - delta)).astype(jnp.bfloat16)
        score_grads.append(d_scores)
        delta_list.append(delta)
        query_grads.append(
            jnp.dot(d_scores, keys_all[:, lower : lower + HEAD], preferred_element_type=jnp.float32)
            * scale
        )
    d_queries = jnp.concatenate(query_grads, axis=1).astype(jnp.bfloat16)
    key_pieces = []
    value_pieces = []
    for head in range(HEADS):
        lower = head * HEAD
        score_part = score_grads[head]
        prob_part = prob_list[head]
        key_pieces.append(rows_product(score_part, queries[:, lower : lower + HEAD]) * scale)
        value_pieces.append(rows_product(prob_part, d_mixed[:, lower : lower + HEAD]))
    key_value_grads = lax.psum_scatter(
        jnp.concatenate(key_pieces + value_pieces, axis=1).astype(jnp.bfloat16),
        "node",
        scatter_dimension=0,
        tiled=True,
    ).astype(jnp.float32)
    d_keys = key_value_grads[:, :width].astype(jnp.bfloat16)
    d_values = key_value_grads[:, width:].astype(jnp.bfloat16)
    normalized_gradient = (
        cols_product(d_queries, query_weight)
        + cols_product(d_keys, key_weight)
        + cols_product(d_values, value_weight)
    )
    node_state_gradient = (
        grads_in.astype(jnp.float32)
        + inverse_norm_scale
        * (
            normalized_gradient
            - centered_states
            * jnp.mean(normalized_gradient * centered_states, axis=1, keepdims=True)
        )
    ).astype(jnp.bfloat16)
    partial_query = rows_product(normalized_states, d_queries)
    partial_key = rows_product(normalized_states, d_keys)
    partial_value = rows_product(normalized_states, d_values)
    total_query, total_key, total_value, total_out = lax.psum(
        (partial_query, partial_key, partial_value, partial_out), ("node", "rep")
    )
    return (
        updated[None],
        node_state_gradient[None],
        total_query,
        total_key,
        total_value,
        total_out,
    )


def solution(mesh):
    in_specs = (
        P(("groups", "rep"), "node", None),
        P(("groups", "rep"), "node", None),
        P(("groups", "rep"), "node", None),
        P(("groups", "rep"), "node"),
        P(("groups", "rep"), None),
        P(),
        P(),
        P(),
        P(),
        P(),
    )
    out_specs = (
        P(("groups", "rep"), "node", None),
        P(("groups", "rep"), "node", None),
        P("groups", None),
        P("groups", None),
        P("groups", None),
        P("groups", None),
    )
    return jax.shard_map(
        on_device, mesh=mesh, in_specs=in_specs, out_specs=out_specs, check_vma=False
    )
```

profile of v0, /device:TPU:0, one launch (start us, length us, event | category | flops | bytes accessed | tf_op | source)
XLA Modules:
  0.0 189.7 jit_solution(12456625626089858018)
XLA Ops:
  7.3 0.6 copy-done.12
  8.0 0.7 copy-done.10
  8.9 0.6 copy-done.13
  9.5 1.0 fusion.42
  11.0 0.6 copy-done.11
  11.6 0.6 convolution_bitcast_fusion
  13.4 0.3 convolution_convert_fusion.3
  13.6 0.3 copy-done.5
  14.1 0.2 convolution_convert_fusion.1
  14.4 15.6 %all_gather.7 = bf16[512,256]{1,0:T(8,128)(2,1)S(1)} all-gather(bf16[128,256]{1,0:T(8,128)(2,1)S(1)} %convolution_convert_fusion.1), channel_id=1, replica_groups=mesh['groups'=2,'node'=4,'rep'=4] {'node'}, dimensions={0}, use_global_device_ids=true | all-gather | bytes 327680 | tf_op jit(solution)/shard_map/all_gather | solution.py:89
  30.0 14.6 %all_gather.6 = bf16[512,256]{1,0:T(8,128)(2,1)S(1)} all-gather(bf16[128,256]{1,0:T(8,128)(2,1)S(1)} %convolution_convert_fusion.2), channel_id=1, replica_groups=mesh['groups'=2,'node'=4,'rep'=4] {'node'}, dimensions={0}, use_global_device_ids=true | all-gather | bytes 327680 | tf_op jit(solution)/shard_map/all_gather | solution.py:88
  44.6 0.4 fusion.46
  45.0 0.4 fusion.43
  45.4 0.3 fusion.124
  45.7 0.4 fusion.127
  46.0 0.4 fusion.44
  46.4 0.3 fusion.126
  46.7 0.4 fusion.45
  47.1 0.4 fusion.125
  47.5 0.4 select_reduce_fusion.3
  47.9 0.3 select_convert_fusion.3
  48.2 0.3 convolution_convert_fusion.10
  48.7 0.3 convolution_convert_fusion.8
  49.0 0.4 copy-done.3
  49.9 0.2 multiply_reduce_fusion.3
  50.3 0.3 fusion.14
  50.8 0.3 fusion.16
  51.3 0.3 fusion.21
  51.8 0.3 fusion.25
  52.7 1.0 copy.27
  54.0 0.3 fusion.31
  54.3 0.3 fusion.33
  54.8 0.2 fusion.105
  55.0 1.0 fusion.50
  56.0 1.1 fusion.104
  57.1 19.4 %reduce-scatter.4.cloned.1.call-done = bf16[128,512]{1,0:T(8,128)(2,1)} async-done(((bf16[512,512]{1,0:T(8,128)(2,1)}), bf16[128,512]{1,0:T(8,128)(2,1)}) %reduce-scatter.4.cloned.1.call-update) | async-done | bytes 131088
  76.5 2.0 %fusion.78 = f32[512,256]{1,0:T(8,128)} fusion(bf16[128,512]{1,0:T(8,128)(2,1)} %reduce-scatter.4.cloned.1.call-done, bf16[1,128,512]{2,1,0:T(8,128)(2,1)S(1)} %copy-done.1, f32[128]{0:T(128)S(1)} %add_rsqrt_fusion), kind=kOutput, calls=%fused_computation.125 | convolution fusion | flops 33751040 | bytes 721408 | tf_op jit(solution)/shard_map/dot_general | solution.py:18
  78.5 1.1 fusion.75
  79.6 0.9 fusion.17
  80.7 0.3 fusion.37
  81.1 0.8 fusion.49
  81.9 95.8 %all-reduce.3.cloned.1.call-done = (f32[512,256]{1,0:T(8,128)}, f32[512,256]{1,0:T(8,128)}, f32[512,256]{1,0:T(8,128)}, f32[256,512]{1,0:T(8,128)}) async-done(((f32[512,256]{1,0:T(8,128)}, f32[512,256]{1,0:T(8,128)}, f32[512,256]{1,0:T(8,128)}, f32[256,512]{1,0:T(8,128)}), (f32[512,256]{1,0:T(8,128)}, f32[512,256]{1,0:T(8,128)}, f32[512,256]{1,0:T(8,128)}, ...) | async-done | bytes 2097168 | tf_op jit(solution)/shard_map/psum | solution.py:183
  177.7 1.9 %copy.53 = f32[512,256]{1,0:T(8,128)} copy(f32[512,256]{1,0:T(8,128)} %get-tuple-element.43) | data formatting | bytes 1048576
  179.6 0.8 copy.54
  180.4 0.4 copy-done.7
  180.8 0.8 copy.55
  181.6 0.4 copy-done.6
  182.0 0.8 copy.56
  (60 shorter events, 5.0 us)
Async XLA Ops:
  7.2 7.0 %copy-start = (bf16[512,256]{1,0:T(8,128)(2,1)S(1)}, bf16[512,256]{1,0:T(8,128)(2,1)}, u32[]{:S(2)}) copy-start(bf16[512,256]{1,0:T(8,128)(2,1)} %param.17) | copy-start | bytes 786436
  7.2 69.3 %reduce-scatter.4.cloned.1.call-start = ((), (), s32[]{:S(2)}) async-start(), calls=%async_computation.1 | async-start | bytes 655360
  7.3 0.7 copy-start.12
  8.0 0.7 copy-start.10
  8.8 0.7 copy-start.13
  10.9 0.7 copy-start.11
  11.6 1.7 copy-start.4
  12.3 1.0 copy-start.1
  12.9 1.0 copy-start.5
  48.5 1.0 copy-start.3
  48.7 0.9 copy-start.2
  53.7 123.9 %all-reduce.3.cloned.1.call-start = ((), (), s32[]{:S(2)}) async-start(), calls=%async_computation.2 | async-start | bytes 4194304 | tf_op jit(solution)/shard_map/psum | solution.py:183
  76.5 2.0 %copy-start.9 = (bf16[128,512]{1,0:T(8,128)(2,1)S(1)}, bf16[128,512]{1,0:T(8,128)(2,1)}, u32[]{:S(2)}) copy-start(bf16[128,512]{1,0:T(8,128)(2,1)} %reduce-scatter.4.cloned.1.call-done) | copy-start | bytes 393220
  177.6 1.9 %copy-start.8 = (f32[512,256]{1,0:T(8,128)S(1)}, f32[512,256]{1,0:T(8,128)}, u32[]{:S(2)}) copy-start(f32[512,256]{1,0:T(8,128)} %get-tuple-element.44) | copy-start | bytes 1572868
  179.6 1.2 copy-start.7
  180.8 1.2 copy-start.6
Sparse Core Ops, SparseCore 0:
  53.8 22.5 reduce-scatter.3
  81.0 96.5 all-reduce.2
where the time goes:
time: 190 us
  waiting for transfers between devices  115 us (61%)
  blocking collectives  30.2 us (16%)
  matrix products  16.7 us (9%)
  between operations  14.3 us (8%)
  local copies, waits for them, and re-layouts  10.3 us (5%)
  other arithmetic  2.95 us (2%)
    psum x1, waiting for transfers between devices, on_device(): lax.psum((partial_query, partial_key, partial_value, partial_out), ('node...  95.8 us
    unnamed x3, waiting for transfers between devices  19.4 us
    all_gather x1, blocking collectives, on_device(): lax.all_gather(values, 'node', axis=0, tiled=True)  15.6 us
    all_gather x1, blocking collectives, on_device(): lax.all_gather(keys, 'node', axis=0, tiled=True)  14.6 us
    unnamed x33, local copies, waits for them, and re-layouts  9.64 us
    dot_general x12, matrix products, rows_product(): lax.dot_general(left, right, CONTRACT_ROWS, preferred_element_type=jnp.fl...  6.81 us
  transfers between devices with their start and end apart: 2, of which 2 were waited for; matrix products, arithmetic and copies ran while one was open for 3% of the time, Pallas kernels for 0%

commit v1 on v0

--- a/solution.py
+++ b/solution.py
@@ -181,7 +181,7 @@
     partial_key = rows_product(normalized_states, d_keys)
     partial_value = rows_product(normalized_states, d_values)
     total_query, total_key, total_value, total_out = lax.psum(
-        (partial_query, partial_key, partial_value, partial_out), ("node", "rep")
+        lax.psum((partial_query, partial_key, partial_value, partial_out), "rep"), "node"
     )
     return (
         updated[None],

time: 190 us -> 233 us (1.23)
  waiting for transfers between devices: 115 us -> 158 us
    psum x1 -> x2, waiting for transfers between devices: 95.8 us -> 139 us  [the longest x1 88.4 us: on_device(): lax.psum(lax.psum((partial_query, partial_key, partial_value, partial_out...]
    unnamed x3 -> x4, waiting for transfers between devices: 19.4 us -> 19.6 us
  transfers between devices with their start and end apart: 2 -> 3, of which waited for: 2 -> 3; matrix products, arithmetic and copies ran while one was open for 3% -> 2% of each run, Pallas kernels for 0% -> 0%
where the time goes in v1:
time: 233 us
  waiting for transfers between devices  158 us (68%)
  blocking collectives  30.2 us (13%)
  matrix products  16.7 us (7%)
  between operations  14.1 us (6%)
  local copies, waits for them, and re-layouts  10.3 us (4%)
  other arithmetic  2.96 us (1%)
    psum x1, waiting for transfers between devices, on_device(): lax.psum(lax.psum((partial_query, partial_key, partial_value, partial_out...  88.4 us
    psum x1, waiting for transfers between devices, on_device(): lax.psum((partial_query, partial_key, partial_value, partial_out), 'rep')  50.3 us
    unnamed x4, waiting for transfers between devices  19.6 us
    all_gather x1, blocking collectives, on_device(): lax.all_gather(values, 'node', axis=0, tiled=True)  15.6 us
    all_gather x1, blocking collectives, on_device(): lax.all_gather(keys, 'node', axis=0, tiled=True)  14.6 us
    unnamed x33, local copies, waits for them, and re-layouts  9.64 us
    dot_general x12, matrix products, rows_product(): lax.dot_general(left, right, CONTRACT_ROWS, preferred_element_type=jnp.fl...  6.82 us
  transfers between devices with their start and end apart: 3, of which 3 were waited for; matrix products, arithmetic and copies ran while one was open for 2% of the time, Pallas kernels for 0%

profile of v1, /device:TPU:0, one launch (start us, length us, event | category | flops | bytes accessed | tf_op | source)
XLA Modules:
  0.0 232.7 jit_solution(12442363032877997024)
XLA Ops:
  7.3 0.6 copy-done.12
  8.0 0.7 copy-done.10
  8.9 0.6 copy-done.13
  9.5 1.0 fusion.42
  11.0 0.6 copy-done.11
  11.6 0.6 convolution_bitcast_fusion
  13.4 0.3 convolution_convert_fusion.3
  13.6 0.3 copy-done.5
  14.1 0.2 convolution_convert_fusion.1
  14.4 15.6 %all_gather.7 = bf16[512,256]{1,0:T(8,128)(2,1)S(1)} all-gather(bf16[128,256]{1,0:T(8,128)(2,1)S(1)} %convolution_convert_fusion.1), channel_id=1, replica_groups=mesh['groups'=2,'node'=4,'rep'=4] {'node'}, dimensions={0}, use_global_device_ids=true | all-gather | bytes 327680 | tf_op jit(solution)/shard_map/all_gather | solution.py:89
  30.0 14.6 %all_gather.6 = bf16[512,256]{1,0:T(8,128)(2,1)S(1)} all-gather(bf16[128,256]{1,0:T(8,128)(2,1)S(1)} %convolution_convert_fusion.2), channel_id=1, replica_groups=mesh['groups'=2,'node'=4,'rep'=4] {'node'}, dimensions={0}, use_global_device_ids=true | all-gather | bytes 327680 | tf_op jit(solution)/shard_map/all_gather | solution.py:88
  44.6 0.4 fusion.46
  45.0 0.4 fusion.43
  45.4 0.3 fusion.124
  45.7 0.4 fusion.127
  46.0 0.4 fusion.44
  46.4 0.3 fusion.126
  46.7 0.4 fusion.45
  47.1 0.4 fusion.125
  47.5 0.4 select_reduce_fusion.3
  47.9 0.3 select_convert_fusion.3
  48.2 0.3 convolution_convert_fusion.10
  48.7 0.3 convolution_convert_fusion.8
  49.0 0.4 copy-done.3
  49.9 0.2 multiply_reduce_fusion.3
  50.3 0.3 fusion.14
  50.8 0.3 fusion.16
  51.3 0.3 fusion.21
  51.8 0.3 fusion.25
  52.7 1.0 copy.27
  54.0 0.3 fusion.31
  54.3 0.3 fusion.33
  54.8 1.0 fusion.50
  55.8 1.1 fusion.104
  56.9 19.6 %reduce-scatter.4.cloned.1.call-done = bf16[128,512]{1,0:T(8,128)(2,1)} async-done(((bf16[512,512]{1,0:T(8,128)(2,1)}), bf16[128,512]{1,0:T(8,128)(2,1)}) %reduce-scatter.4.cloned.1.call-update) | async-done | bytes 131088
  76.5 2.0 fusion.78
  78.5 1.1 fusion.75
  79.7 50.3 %all-reduce.5.cloned.1.call-done = (f32[512,256]{1,0:T(8,128)}, f32[512,256]{1,0:T(8,128)}, f32[512,256]{1,0:T(8,128)}, f32[256,512]{1,0:T(8,128)}) async-done(((f32[512,256]{1,0:T(8,128)}, f32[512,256]{1,0:T(8,128)}, f32[512,256]{1,0:T(8,128)}, f32[256,512]{1,0:T(8,128)}), (f32[512,256]{1,0:T(8,128)}, f32[512,256]{1,0:T(8,128)}, f32[512,256]{1,0:T(8,128)}, ...) | async-done | bytes 2097168 | tf_op jit(solution)/shard_map/psum | solution.py:184
  130.0 0.9 fusion.17
  131.4 0.3 fusion.37
  131.7 0.8 fusion.49
  132.5 88.4 %all-reduce.7.cloned.1.call-done = (f32[512,256]{1,0:T(8,128)}, f32[512,256]{1,0:T(8,128)}, f32[512,256]{1,0:T(8,128)}, f32[256,512]{1,0:T(8,128)}) async-done(((f32[512,256]{1,0:T(8,128)}, f32[512,256]{1,0:T(8,128)}, f32[512,256]{1,0:T(8,128)}, f32[256,512]{1,0:T(8,128)}), (f32[512,256]{1,0:T(8,128)}, f32[512,256]{1,0:T(8,128)}, f32[512,256]{1,0:T(8,128)}, ...) | async-done | bytes 2097168 | tf_op jit(solution)/shard_map/psum | solution.py:183
  220.9 1.9 copy.57
  222.9 0.8 copy.58
  223.7 0.4 copy-done.7
  224.1 0.8 copy.59
  224.9 0.4 copy-done.6
  225.3 0.8 copy.60
  (63 shorter events, 5.3 us)
Async XLA Ops:
  7.2 7.0 %copy-start = (bf16[512,256]{1,0:T(8,128)(2,1)S(1)}, bf16[512,256]{1,0:T(8,128)(2,1)}, u32[]{:S(2)}) copy-start(bf16[512,256]{1,0:T(8,128)(2,1)} %param.17) | copy-start | bytes 786436
  7.2 69.3 %reduce-scatter.4.cloned.1.call-start = ((), (), s32[]{:S(2)}) async-start(), calls=%async_computation.1 | async-start | bytes 655360
  7.3 0.7 copy-start.12
  8.0 0.7 copy-start.10
  8.8 0.7 copy-start.13
  10.9 0.7 copy-start.11
  11.6 1.7 copy-start.4
  12.3 1.0 copy-start.1
  12.9 1.0 copy-start.5
  48.5 1.0 copy-start.3
  48.7 0.9 copy-start.2
  53.7 76.3 %all-reduce.5.cloned.1.call-start = ((), (), s32[]{:S(2)}) async-start(), calls=%async_computation.2 | async-start | bytes 4194304 | tf_op jit(solution)/shard_map/psum | solution.py:184
  76.5 2.0 copy-start.9
  79.6 141.3 %all-reduce.7.cloned.1.call-start = ((), (), s32[]{:S(2)}) async-start(), calls=%async_computation.3 | async-start | bytes 4194304 | tf_op jit(solution)/shard_map/psum | solution.py:183
  220.9 1.9 copy-start.8
  222.9 1.2 copy-start.7
  224.1 1.2 copy-start.6
Sparse Core Ops, SparseCore 0:
  53.8 22.5 reduce-scatter.3
  79.8 50.2 all-reduce.4
  132.8 88.0 all-reduce.6
